TPU v7x, 128 devices: a whole 4x4x4 slice. The times are simulated.
128 devices in a mesh: member: 8 (over y, core), fsdp: 16 (over z, x).
Axes of the slice: x: 4, y: 4, z: 4, core: 2. Of those that a mesh axis runs over, the one named last changes fastest.
Arguments:
- tokens: bfloat16 [3072, 4096], P('fsdp'), may hold values from -6 to 6
- routes: int32 [3072, 2], P('fsdp'), may hold values from 0 to 7, all different within a row; in each aligned block of 192 rows (0 to 191, 192 to 383, ...) at most 72 rows name the same one
- combine: float32 [3072, 2], P('fsdp'), may hold values from 0.25 to 1
- gate_weight: bfloat16 [8, 11008, 4096], P('member', None, 'fsdp'), may hold values from -0.09375 to 0.09375
- up_weight: bfloat16 [8, 11008, 4096], P('member', None, 'fsdp'), may hold values from -0.09375 to 0.09375
- down_weight: bfloat16 [8, 11008, 4096], P('member', None, 'fsdp'), may hold values from -0.0546875 to 0.0546875
Outputs:
- mixed: bfloat16 [3072, 4096], P('fsdp', 'member')
Inputs may be any that keep to these rules, and one draw needn't show every extreme that they name: `routes`: each row names two different experts. In each aligned block of 192 rows no expert is named by more than 72 rows, a bound that some block reaches.
All inputs are finite; a program needn't handle non-finite values.
Results may differ from a plain program's by a relative error of at most 0.0049.
Values may be sent and summed in bfloat16 or wider, within the bound.
A program may use at most 128 MiB of HBM per device.

v0:
```python
import jax
import jax.numpy as jnp
from jax import lax
from jax.sharding import PartitionSpec as P


def blocked(weight, groups):
    return weight.reshape(groups, weight.shape[1] // groups, weight.shape[2])


def body(tokens, routes, combine, gate_weight, up_weight, down_weight):
    expert = lax.axis_index("member")
    groups = lax.axis_size("fsdp")
    tok_rows = tokens.shape[0]
    capacity = 3 * tok_rows // lax.axis_size("member")
    picked = routes == expert
    chosen = jnp.any(picked, axis=1)
    token_weight = jnp.sum(jnp.where(picked, combine, jnp.zeros_like(combine)), axis=1)
    position = jnp.cumsum(chosen.astype(jnp.int32)) - 1
    slot_ids = jnp.arange(capacity, dtype=jnp.int32)
    placed = (position[:, None] == slot_ids[None, :]) & chosen[:, None]
    packed = lax.dot_general(
        placed.astype(jnp.bfloat16),
        tokens,
        (((0,), (0,)), ((), ())),
        preferred_element_type=jnp.float32,
    ).astype(jnp.bfloat16)
    gate_local, up_local, down_moved = (
        lax.all_to_all(
            blocked(gate_weight, groups), "fsdp", split_axis=0, concat_axis=0, tiled=True
        ),
        lax.all_to_all(blocked(up_weight, groups), "fsdp", split_axis=0, concat_axis=0, tiled=True),
        lax.all_to_all(
            blocked(down_weight, groups), "fsdp", split_axis=0, concat_axis=0, tiled=True
        ),
    )
    feat_part = gate_local.shape[2]
    piece = lax.all_gather(packed, "fsdp", axis=0, tiled=True)
    split_rows = piece.reshape(piece.shape[0], groups, feat_part)
    gate_act = lax.dot_general(
        split_rows, gate_local, (((1, 2), (0, 2)), ((), ())), preferred_element_type=jnp.float32
    )
    up_act = lax.dot_general(
        split_rows, up_local, (((1, 2), (0, 2)), ((), ())), preferred_element_type=jnp.float32
    )
    hidden = (jax.nn.silu(gate_act) * up_act).astype(jnp.bfloat16)
    result = lax.dot_general(
        hidden, down_moved, (((1,), (1,)), ((), ())), preferred_element_type=jnp.float32
    )
    expert_out = lax.psum_scatter(
        result.reshape(capacity * lax.axis_size("fsdp"), groups * feat_part),
        "fsdp",
        scatter_dimension=0,
        tiled=True,
    )
    spread = jnp.where(placed, token_weight[:, None], jnp.zeros_like(token_weight[:, None]))
    weighted = jnp.dot(
        spread, expert_out, precision=lax.Precision.HIGHEST, preferred_element_type=jnp.float32
    )
    mixed = lax.psum_scatter(weighted, "member", scatter_dimension=1, tiled=True)
    return mixed.astype(jnp.bfloat16)


def solution(mesh):
    placed = (
        P("fsdp", None),
        P("fsdp", None),
        P("fsdp", None),
        P("member", None, "fsdp"),
        P("member", None, "fsdp"),
        P("member", None, "fsdp"),
    )
    return jax.shard_map(
        body, mesh=mesh, in_specs=placed, out_specs=P("fsdp", "member"), check_vma=False
    )
```

profile of v0, /device:TPU:0, one launch (start us, length us, event | category | flops | bytes accessed | tf_op | source)
XLA Modules:
  0.0 591.8 jit_solution(9888366151032046023)
XLA Ops:
  6.5 0.0 copy-start
  6.5 0.0 all-gather.2.cloned.1.call-start
  6.5 0.8 fusion.36
  7.4 0.3 reduce-window.9
  7.7 0.1 slice.10
  7.8 0.1 slice_reduce_fusion
  7.9 0.1 add_bitcast_fusion
  8.0 0.0 copy-done
  8.0 1.4 convolution_convert_fusion
  9.4 0.0 slice-start
  9.4 0.0 all-gather.2.cloned.1.call-update
  9.4 0.0 slice-start.1
  9.4 84.2 %all_to_all.15 = bf16[16,688,256]{2,1,0:T(8,128)(2,1)} all-to-all(bf16[16,688,256]{2,1,0:T(8,128)(2,1)} %bitcast.45), channel_id=1, replica_groups=mesh['member'=8,'fsdp'=16] {'fsdp'}, dimensions={0} | all-to-all | bytes 11272192 | tf_op jit(solution)/shard_map/all_to_all | solution.py:29
  93.6 0.0 slice-done
  93.6 0.0 slice-done.1
  93.6 106.9 %all_to_all.16 = bf16[16,688,256]{2,1,0:T(8,128)(2,1)} all-to-all(bf16[16,688,256]{2,1,0:T(8,128)(2,1)S(1)} %bitcast.48), channel_id=1, replica_groups=mesh['member'=8,'fsdp'=16] {'fsdp'}, dimensions={0} | all-to-all | bytes 11272192 | tf_op jit(solution)/shard_map/all_to_all | solution.py:32
  200.5 0.0 slice-start.2
  200.5 4.7 all-to-all-start.2
  205.2 0.0 all-reduce.4.cloned.1.call-start
  205.3 0.0 all-gather.2.cloned.1.call-done
  205.3 0.0 slice-start.3
  205.3 0.0 copy-start.4
  205.3 11.1 %fusion.6 = f32[1152,688]{0,1:T(8,128)S(1)} fusion(bf16[16,688,256]{2,1,0:T(8,128)(2,1)} %all_to_all.15, bf16[144,16,8,256]{3,2,1,0:T(8,128)(2,1)} %bitcast.52), kind=kOutput, calls=%fused_computation.7 | convolution fusion | flops 6492782592 | bytes 18243584 | tf_op jit(solution)/shard_map/dot_general | solution.py:40
  216.4 0.0 slice-done.2
  216.4 0.0 slice-done.3
  216.4 0.0 copy-done.4
  216.4 9.1 %fusion.18 = bf16[1152,688,1]{0,1,2:T(8,128)(2,1)} fusion(bf16[16,688,256]{2,1,0:T(8,128)(2,1)S(1)} %bitcast.51, bf16[144,16,8,256]{3,2,1,0:T(8,128)(2,1)S(1)} %bitcast.53, f32[1152,688]{0,1:T(8,128)S(1)} %fusion.6), kind=kOutput, calls=%fused_computation.11 | convolution fusion | flops 6497538048 | bytes 19828736 | tf_op jit(solution)/shard_map/dot_general | solution.py:43
  225.5 59.8 %all-to-all-done.2 = bf16[16,688,256]{2,1,0:T(8,128)(2,1)} async-done(((bf16[16,688,256]{2,1,0:T(8,128)(2,1)}), bf16[16,688,256]{2,1,0:T(8,128)(2,1)}, u32[]{:S(2)}, u32[]{:S(2)}) %all-to-all-start.2) | async-done | bytes 5636128 | tf_op jit(solution)/shard_map/all_to_all | solution.py:33
  285.4 14.4 %fusion.37 = f32[1152,16,256]{0,2,1:T(8,128)} fusion(bf16[1152,688,1]{0,1,2:T(8,128)(2,1)} %fusion.18, bf16[16,688,256]{2,1,0:T(8,128)(2,1)} %all-to-all-done.2), kind=kOutput, calls=%fused_computation.33 | convolution fusion | flops 6492782592 | bytes 26095616 | tf_op jit(solution)/shard_map/dot_general | solution.py:47
  299.7 0.0 copy-start.5
  299.7 0.0 copy-start.2
  299.7 0.0 copy-start.3
  299.8 0.0 all-reduce.4.cloned.1.call-update
  299.8 0.0 copy-start.1
  299.8 0.2 reduce-scatter.3.cloned.1.call-start
  300.0 0.4 copy-done.5
  300.4 0.6 dynamic-slice
  301.6 0.0 copy-done.2
  301.6 0.0 copy-done.3
  301.7 239.3 %all-reduce.4.cloned.1.call-done = f32[1152,4096]{0,1:T(8,128)} async-done(((f32[1152,4096]{0,1:T(8,128)}), f32[1152,4096]{0,1:T(8,128)}) %all-reduce.4.cloned.1.call-update) | async-done | bytes 18874384
  541.0 6.8 %fusion.21 = f32[192,4096]{1,0:T(8,128)} fusion(f32[1152,4096]{0,1:T(8,128)} %all-reduce.4.cloned.1.call-done, u32[]{:T(128)S(6)} %multiply.1, f32[192]{0:T(256)S(1)} %select_reduce_fusion, s32[192]{0:T(256)S(1)} %slice_add_fusion, pred[192]{0:T(512)(128)(4,1)S(1)} %fusion.36), kind=kOutput, calls=%fused_computation.12 | convolution fusion | flops 679518720 | bytes 5244612 | tf_op jit(solution)/shard_map/dot_general | solution.py:57
  547.8 0.0 reduce-scatter.3.cloned.1.call-update
  547.8 35.8 %reduce-scatter.3.cloned.1.call-done = f32[192,512]{1,0:T(8,128)} async-done(((f32[192,4096]{1,0:T(8,128)}), f32[192,512]{1,0:T(8,128)}) %reduce-scatter.3.cloned.1.call-update) | async-done | bytes 393232 | tf_op jit(solution)/shard_map/reduce_scatter | solution.py:60
  583.6 1.7 convert_element_type.13
  585.3 0.0 copy-done.1
  (6 shorter events, 0.1 us)
Async XLA Ops:
  6.5 1.5 copy-start
  6.5 198.7 %all-gather.2.cloned.1.call-start = ((), (), s32[]{:S(2)}) async-start(), calls=%async_computation.4 | async-start | bytes 10027008 | tf_op jit(solution)/shard_map/all_gather | solution.py:38
  9.4 84.2 %slice-start = ((s8[5636096]{0:T(1024)(128)(4,1)}), s8[1441792]{0:T(1024)(128)(4,1)S(1)}, s32[]{:S(2)}) async-start(s8[5636096]{0:T(1024)(128)(4,1)} %bitcast.46), calls=%async_computation.7 | async-start | bytes 2883584
  9.4 84.2 %slice-start.1 = ((s8[5636096]{0:T(1024)(128)(4,1)}), s8[4194304]{0:T(1024)(128)(4,1)S(1)}, s32[]{:S(2)}) async-start(s8[5636096]{0:T(1024)(128)(4,1)} %bitcast.46), calls=%async_computation.8 | async-start | bytes 8388608
  200.5 15.9 %slice-start.2 = ((s8[5636096]{0:T(1024)(128)(4,1)}), s8[1441792]{0:T(1024)(128)(4,1)S(1)}, s32[]{:S(2)}) async-start(s8[5636096]{0:T(1024)(128)(4,1)} %bitcast.50), calls=%async_computation.9 | async-start | bytes 2883584
  200.5 84.9 %all-to-all-start.2 = ((bf16[16,688,256]{2,1,0:T(8,128)(2,1)}), bf16[16,688,256]{2,1,0:T(8,128)(2,1)}, u32[]{:S(2)}, u32[]{:S(2)}) async-start(bf16[16,688,256]{2,1,0:T(8,128)(2,1)} %bitcast.49), calls=%async_computation.2 | async-start | bytes 11272192 | tf_op jit(solution)/shard_map/all_to_all | solution.py:33
  205.2 335.8 %all-reduce.4.cloned.1.call-start = ((), (), s32[]{:S(2)}) async-start(), calls=%async_computation.6 | async-start | bytes 37748736
  205.3 11.1 %slice-start.3 = ((s8[5636096]{0:T(1024)(128)(4,1)}), s8[4194304]{0:T(1024)(128)(4,1)S(1)}, s32[]{:S(2)}) async-start(s8[5636096]{0:T(1024)(128)(4,1)} %bitcast.50), calls=%async_computation.10 | async-start | bytes 8388608
  205.3 11.1 %copy-start.4 = (bf16[1152,4096]{1,0:T(8,128)(2,1)S(1)}, bf16[1152,4096]{1,0:T(8,128)(2,1)}, u32[]{:S(2)}) copy-start(bf16[1152,4096]{1,0:T(8,128)(2,1)} %all-gather.2.cloned.1.call-done) | copy-start | bytes 28311556
  299.7 0.7 copy-start.5
  299.7 1.9 copy-start.2
  299.7 1.9 copy-start.3
  299.8 285.5 %copy-start.1 = (bf16[192,4096]{1,0:T(8,128)(2,1)S(1)}, bf16[192,4096]{1,0:T(8,128)(2,1)}, u32[]{:S(2)}) copy-start(bf16[192,4096]{1,0:T(8,128)(2,1)} %param.6) | copy-start | bytes 4718596
  299.8 283.8 %reduce-scatter.3.cloned.1.call-start = ((), (), s32[]{:S(2)}) async-start(), calls=%async_computation.5 | async-start | bytes 3538944 | tf_op jit(solution)/shard_map/reduce_scatter | solution.py:60
Sparse Core Ops, SparseCore 0:
  9.5 188.3 all-gather.1
  299.9 241.0 all-reduce.3
  548.0 35.5 reduce-scatter.2
where the time goes:
time: 592 us
  waiting for transfers between devices  335 us (57%)
  blocking collectives  191 us (32%)
  matrix products  42.8 us (7%)
  between operations  13.9 us (2%)
    unnamed x4, waiting for transfers between devices  239 us
    all_to_all x1, blocking collectives, body(): lax.all_to_all(blocked(up_weight, groups), 'fsdp', split_axis=0, concat_a...  107 us
    all_to_all x1, blocking collectives, body(): lax.all_to_all(blocked(gate_weight, groups), 'fsdp', split_axis=0, concat...  84.2 us
    all_to_all x1, waiting for transfers between devices, body(): lax.all_to_all(blocked(down_weight, groups), 'fsdp', split_axis=0, concat...  59.8 us
    reduce_scatter x1, waiting for transfers between devices, body(): lax.psum_scatter(weighted, 'member', scatter_dimension=1, tiled=True)  35.8 us
    dot_general x1, matrix products, body(): lax.dot_general(hidden, down_moved, (((1,), (1,)), ((), ())), preferred_e...  14.4 us
  transfers between devices with their start and end apart: 4, of which 3 were waited for; matrix products, arithmetic and copies ran while one was open for 4% of the time, Pallas kernels for 0%

commit v1 on v0

v1 whole, which is shorter than its diff:
```python
import jax
import jax.numpy as jnp
from jax import lax
from jax.experimental import pallas as pl
from jax.experimental.pallas import tpu as pltpu
from jax.sharding import PartitionSpec as P

PIECE = 256
AHEAD = 3
MESH = pl.DeviceIdType.MESH


def contract(a, b, dims):
    return lax.dot_general(a, b, (dims, ((), ())), preferred_element_type=jnp.float32)


def kernel(
    packed, gate, up, down, out,
    tokbuf, tok, acc, wgu, wd, ps, pr, own, hb, osb, orv, fin, frv,
    tok_s, tok_r, gu_s, gu_r, d_s, d_r, p_s, p_r, h_s, h_r, o_s, o_r, f_s, f_r,
):
    steps = wgu.shape[0]
    slots = packed.shape[0]
    wide = tok.shape[1]
    group = tok.shape[0] // 4
    half = out.shape[2]
    me = lax.axis_index("member")
    shard = lax.axis_index("fsdp")
    z, x = shard // 4, shard % 4

    def first_row(xt):
        return xt * (steps * PIECE) - (xt // 3) * (4 * steps * PIECE - gate.shape[0])

    def wait(ref, sem):
        pltpu.make_async_copy(ref, ref, sem).wait()

    def columns(zt):
        return packed.at[:, pl.ds(pl.multiple_of(zt * wide, wide), wide)]

    def send_gate_up(c):
        for dx in (2, 1, 3):
            xt = (x + dx) % 4
            rows = pl.ds(pl.multiple_of(first_row(xt) + c * PIECE, PIECE), PIECE)
            for w, ref in enumerate((gate, up)):
                pltpu.make_async_remote_copy(
                    ref.at[rows], wgu.at[c, x, w], gu_s.at[c], gu_r.at[c],
                    device_id={"fsdp": z * 4 + xt}, device_id_type=MESH,
                ).start()
        rows = pl.ds(pl.multiple_of(first_row(x) + c * PIECE, PIECE), PIECE)
        for w, ref in enumerate((gate, up)):
            pltpu.make_async_copy(ref.at[rows], wgu.at[c, x, w], gu_r.at[c]).start()

    def send_down(c):
        for dx in (2, 1, 3):
            xt = (x + dx) % 4
            rows = pl.ds(pl.multiple_of(first_row(xt) + c * PIECE, PIECE), PIECE)
            pltpu.make_async_remote_copy(
                down.at[rows], wd.at[c, x], d_s.at[c], d_r.at[c],
                device_id={"fsdp": z * 4 + xt}, device_id_type=MESH,
            ).start()
        rows = pl.ds(pl.multiple_of(first_row(x) + c * PIECE, PIECE), PIECE)
        pltpu.make_async_copy(down.at[rows], wd.at[c, x], d_r.at[c]).start()

    for hop in range(1, 16):
        other = (shard + hop) % 16
        pltpu.make_async_remote_copy(
            columns(other // 4), tokbuf.at[shard], tok_s.at[hop], tok_r.at[shard],
            device_id={"fsdp": other}, device_id_type=MESH,
        ).start()
    pltpu.make_async_copy(columns(z), tokbuf.at[shard], tok_r.at[shard]).start()
    for c in range(AHEAD):
        send_gate_up(c)

    for f in range(16):
        wait(tokbuf.at[f], tok_r.at[f])
        acc[pl.ds(f * slots, slots), :] = tokbuf[f].astype(jnp.float32)
    for g in range(4):
        rows = pl.ds(g * group, group)
        tok[rows, :] = acc[rows, :].astype(tok.dtype)
    acc[...] = jnp.zeros_like(acc)

    def partial_sums(i):
        slot = i % 4
        wait(wgu.at[i], gu_r.at[i])

        @pl.when(i >= 4)
        def _():
            wait(ps.at[slot], p_s.at[i - 4])

        for dz in (2, 1, 3, 0):
            zt = (z + dz) % 4
            rows = pl.ds(pl.multiple_of(zt * group, 16), group)
            for w in range(2):
                total = contract(tok[rows, 0:PIECE], wgu[i, 0, w], ((1,), (1,)))
                for k in range(1, 4):
                    total += contract(
                        tok[rows, k * PIECE : (k + 1) * PIECE], wgu[i, k, w], ((1,), (1,))
                    )
                if dz:
                    ps[slot, dz - 1, w] = total.astype(ps.dtype)
                else:
                    own[i % 2, w] = total
            if dz:
                pltpu.make_async_remote_copy(
                    ps.at[slot, dz - 1], pr.at[i, dz - 1], p_s.at[i], p_r.at[i],
                    device_id={"fsdp": zt * 4 + x}, device_id_type=MESH,
                ).start()

    def activate(j):
        wait(pr.at[j], p_r.at[j])
        sums = []
        for w in range(2):
            total = own[j % 2, w]
            for s in range(3):
                total += pr[j, s, w].astype(jnp.float32)
            sums.append(total)
        hidden = sums[0] / (1.0 + jnp.exp(-sums[0])) * sums[1]
        twice = jnp.logical_and(x == 3, j * PIECE < 4 * steps * PIECE - gate.shape[0])
        hidden = jnp.where(twice, jnp.zeros_like(hidden), hidden)
        hb[j, z] = hidden.astype(hb.dtype)
        for dz in (2, 1, 3):
            pltpu.make_async_remote_copy(
                hb.at[j, z], hb.at[j, z], h_s.at[j], h_r.at[j],
                device_id={"fsdp": ((z + dz) % 4) * 4 + x}, device_id_type=MESH,
            ).start()

    def project(k):
        wait(hb.at[k, 0:3], h_r.at[k])
        wait(wd.at[k], d_r.at[k])
        for g in range(4):
            rows = pl.ds(g * group, group)
            for b in range(4):
                cols = slice(b * PIECE, (b + 1) * PIECE)
                acc[rows, cols] += contract(hb[k, g], wd[k, b], ((1,), (0,)))

    def step(i, carry):
        @pl.when(i + AHEAD < steps)
        def _():
            send_gate_up(i + AHEAD)

        @pl.when(i < steps)
        def _():
            send_down(i)
            partial_sums(i)

        @pl.when(jnp.logical_and(i >= 1, i < steps + 1))
        def _():
            activate(i - 1)

        @pl.when(i >= 2)
        def _():
            project(i - 2)

        return carry

    lax.fori_loop(0, steps + 2, step, 0)

    for dx in (2, 1, 3):
        xt = (x + dx) % 4
        for zb in range(4):
            rows = pl.ds(pl.multiple_of((zb * 4 + xt) * slots, 8), slots)
            osb[dx - 1, zb] = acc[rows, :].astype(osb.dtype)
        pltpu.make_async_remote_copy(
            osb.at[dx - 1], orv.at[dx - 1], o_s.at[dx - 1], o_r.at[dx - 1],
            device_id={"fsdp": z * 4 + xt}, device_id_type=MESH,
        ).start()
    for s in range(3):
        wait(orv.at[s], o_r.at[s])
    for zb in range(4):
        rows = pl.ds(pl.multiple_of((zb * 4 + x) * slots, 8), slots)
        total = acc[rows, :]
        for s in range(3):
            total += orv[s, zb].astype(jnp.float32)
        for h in range(2):
            fin[zb, h] = total[:, h * half : (h + 1) * half].astype(fin.dtype)
    for zb in range(4):
        for h in range(2):
            here = jnp.logical_and(me == 2 * z + h, zb == z)

            @pl.when(jnp.logical_not(here))
            def _():
                copy = pltpu.make_async_remote_copy(
                    fin.at[zb, h], frv.at[me], f_s.at[zb * 2 + h], f_r.at[me],
                    device_id={"member": 2 * z + h, "fsdp": zb * 4 + x}, device_id_type=MESH,
                )
                copy.start()

            @pl.when(here)
            def _():
                pltpu.make_async_copy(fin.at[zb, h], frv.at[me], f_r.at[me]).start()

    for m in range(8):
        wait(frv.at[m], f_r.at[m])
        out[m] = frv[m]

    for zb in range(4):
        for h in range(2):
            @pl.when(jnp.logical_not(jnp.logical_and(me == 2 * z + h, zb == z)))
            def _():
                wait(fin.at[zb, h], f_s.at[zb * 2 + h])

    for s in range(3):
        wait(osb.at[s], o_s.at[s])
    for hop in range(1, 16):
        wait(tokbuf.at[0], tok_s.at[hop])

    def finish(c, carry):
        wait(wgu.at[c, 0:3], gu_s.at[c])
        wait(wd.at[c, 0:3], d_s.at[c])
        wait(hb.at[c, 0:3], h_s.at[c])

        @pl.when(c >= steps - 4)
        def _():
            wait(ps.at[c % 4], p_s.at[c])

        return carry

    lax.fori_loop(0, steps, finish, 0)


def exchange(packed, gate, up, down):
    slots, wide = packed.shape[0], packed.shape[1] // 4
    rows = 16 * slots
    steps = -(-gate.shape[0] // (4 * PIECE))
    half = packed.shape[1] // 8
    bf16, f32 = jnp.bfloat16, jnp.float32
    dma = pltpu.SemaphoreType.DMA
    return pl.pallas_call(
        kernel,
        out_shape=jax.ShapeDtypeStruct((8, slots, half), bf16),
        in_specs=[pl.BlockSpec(memory_space=pl.ANY)] * 4,
        out_specs=pl.BlockSpec(memory_space=pltpu.VMEM),
        scratch_shapes=[
            pltpu.VMEM((16, slots, wide), bf16),
            pltpu.VMEM((rows, wide), bf16),
            pltpu.VMEM((rows, wide), f32),
            pltpu.VMEM((steps, 4, 2, PIECE, PIECE), bf16),
            pltpu.VMEM((steps, 4, PIECE, PIECE), bf16),
            pltpu.VMEM((4, 3, 2, rows // 4, PIECE), bf16),
            pltpu.VMEM((steps, 3, 2, rows // 4, PIECE), bf16),
            pltpu.VMEM((2, 2, rows // 4, PIECE), f32),
            pltpu.VMEM((steps, 4, rows // 4, PIECE), bf16),
            pltpu.VMEM((3, 4, slots, wide), bf16),
            pltpu.VMEM((3, 4, slots, wide), bf16),
            pltpu.VMEM((4, 2, slots, half), bf16),
            pltpu.VMEM((8, slots, half), bf16),
            dma((16,)), dma((16,)),
            dma((steps,)), dma((steps,)), dma((steps,)), dma((steps,)),
            dma((steps,)), dma((steps,)), dma((steps,)), dma((steps,)),
            dma((3,)), dma((3,)), dma((8,)), dma((8,)),
        ],
        compiler_params=pltpu.CompilerParams(
            has_side_effects=True, vmem_limit_bytes=67043328
        ),
    )(packed, gate, up, down)


def body(tokens, routes, combine, gate_weight, up_weight, down_weight):
    expert = lax.axis_index("member")
    experts = lax.axis_size("member")
    slots = 3 * tokens.shape[0] // experts
    ids = jnp.arange(experts, dtype=routes.dtype)
    named = routes[:, :, None] == ids[None, None, :]
    chosen = jnp.any(named, axis=1)
    order = jnp.cumsum(chosen.astype(jnp.int32), axis=0) - 1
    slot_ids = jnp.arange(slots, dtype=jnp.int32)
    mine = jnp.any(routes == expert, axis=1)
    position = jnp.sum(jnp.where(ids[None, :] == expert, order, 0), axis=1)
    placed = (position[:, None] == slot_ids[None, :]) & mine[:, None]
    packed = lax.dot_general(
        placed.astype(jnp.bfloat16), tokens, (((0,), (0,)), ((), ())),
        preferred_element_type=jnp.float32,
    ).astype(jnp.bfloat16)
    parts = exchange(packed, gate_weight[0], up_weight[0], down_weight[0])
    place = jnp.sum(jnp.where(named, (order + ids[None, :] * slots)[:, None, :], 0), axis=2)
    rows = parts.reshape(experts * slots, parts.shape[2])
    all_ids = jnp.arange(experts * slots, dtype=jnp.int32)
    mixed = 0.0
    for k in range(routes.shape[1]):
        pick = (place[:, k][:, None] == all_ids[None, :]).astype(jnp.bfloat16)
        mixed += combine[:, k][:, None] * jnp.dot(
            pick, rows, preferred_element_type=jnp.float32
        )
    return mixed.astype(jnp.bfloat16)


def solution(mesh):
    placed = (
        P("fsdp", None),
        P("fsdp", None),
        P("fsdp", None),
        P("member", None, "fsdp"),
        P("member", None, "fsdp"),
        P("member", None, "fsdp"),
    )
    return jax.shard_map(
        body, mesh=mesh, in_specs=placed, out_specs=P("fsdp", "member"), check_vma=False
    )
```

time: 592 us -> 338 us (0.57)
  waiting for transfers between devices: 335 us -> 0 us
  Pallas kernels: 0 us -> 323 us
  blocking collectives: 191 us -> 0 us
  matrix products: 42.8 us -> 6.29 us
  between operations: 13.9 us -> 0.04 us
    pallas_call x0 -> x1, Pallas kernels: none -> 323 us  [exchange(): pl.pallas_call(kernel, out_shape=jax.ShapeDtypeStruct((8, slots, half), b...]
    unnamed x4 -> x0, waiting for transfers between devices: 239 us -> none
    all_to_all x2 -> x0, blocking collectives: 191 us -> none  [the longest x1 107 us: body(): lax.all_to_all(blocked(up_weight, groups), 'fsdp', split_axis=0, concat_a...]
    all_to_all x1 -> x0, waiting for transfers between devices: 59.8 us -> none  [body(): lax.all_to_all(blocked(down_weight, groups), 'fsdp', split_axis=0, concat...]
    dot_general x4 -> x2, matrix products: 41.4 us -> 3.55 us  [body(): jnp.dot(pick, rows, preferred_element_type=jnp.float32)]
    reduce_scatter x1 -> x0, waiting for transfers between devices: 35.8 us -> none  [body(): lax.psum_scatter(weighted, 'member', scatter_dimension=1, tiled=True)]
  transfers between devices with their start and end apart: 4 -> 0, of which waited for: 3 -> 0; matrix products, arithmetic and copies ran while one was open for 4% -> 0% of each run, Pallas kernels for 0% -> 0%
where the time goes in v1:
time: 338 us; the launch traced here: 335 us
  Pallas kernels  323 us (96%)
  matrix products  6.29 us (2%)
    pallas_call x1, Pallas kernels, exchange(): pl.pallas_call(kernel, out_shape=jax.ShapeDtypeStruct((8, slots, half), b...  323 us

profile of v1, /device:TPU:0, one launch (start us, length us, event | category | flops | bytes accessed | tf_op | source)
XLA Modules:
  0.0 334.7 jit_solution(4719810369021855604)
XLA Ops:
  0.0 0.7 compare_reduce_fusion
  0.7 0.7 fusion.8
  1.4 1.3 fusion.10
  2.7 0.6 reduce-window.6
  3.3 0.2 slice_reduce_fusion
  3.6 0.1 add_bitcast_fusion
  3.7 0.1 fusion.9
  3.8 0.7 select_reduce_fusion
  4.5 0.6 fusion.11
  5.0 2.7 convolution_convert_fusion.packed
  7.8 323.4 %shard_map.64 = bf16[8,72,512]{2,1,0:T(8,128)(2,1)} custom-call(bf16[72,4096]{1,0:T(8,128)(2,1)} %convolution_convert_fusion.packed, bf16[11008,256]{1,0:T(8,128)(2,1)} %bitcast.18, bf16[11008,256]{1,0:T(8,128)(2,1)} %bitcast.19, bf16[11008,256]{1,0:T(8,128)(2,1)} %bitcast.20), custom_call_target="tpu_custom_call" | custom-call | tf_op jit(solution)/shard_map/pallas_call | solution.py:228
  331.2 1.4 convolution_multiply_fusion
  332.6 2.1 fusion.1
  (5 shorter events, 0.1 us)

commit v2 on v1

v2 whole, which is shorter than its diff:
```python
import jax
import jax.numpy as jnp
from jax import lax
from jax.experimental import pallas as pl
from jax.experimental.pallas import tpu as pltpu
from jax.sharding import PartitionSpec as P

PIECE = 256
AHEAD = 3
MESH = pl.DeviceIdType.MESH


def contract(a, b, dims):
    return lax.dot_general(a, b, (dims, ((), ())), preferred_element_type=jnp.float32)


def kernel(
    tokens, routes, combine, gate, up, down, out,
    tokv, packed, tokbuf, tok, acc, wgu, wd, ps, rl, pr, own, keep, hb, osb, orv, fin, frv,
    t_c, tok_s, tok_r, gu_s, gu_r, d_s, d_r, p_s, l_r, p_r, h_s, h_r, o_s, o_r, f_s, f_r,
):
    steps = wgu.shape[0]
    slots = packed.shape[0]
    wide = tok.shape[1]
    group = tok.shape[0] // 4
    half = out.shape[1]
    count = tokv.shape[0]
    me = lax.axis_index("member")
    shard = lax.axis_index("fsdp")
    z, x = shard // 4, shard % 4

    def first_row(xt):
        return xt * (steps * PIECE) - (xt // 3) * (4 * steps * PIECE - gate.shape[0])

    def wait(ref, sem):
        pltpu.make_async_copy(ref, ref, sem).wait()

    def remote(src, dst, send, recv, zt, xt):
        pltpu.make_async_remote_copy(
            src, dst, send, recv, device_id={"fsdp": zt * 4 + xt}, device_id_type=MESH
        ).start()

    def columns(zt):
        return packed.at[:, pl.ds(pl.multiple_of(zt * wide, wide), wide)]

    def send_gate_up(c):
        for dx in (2, 1, 3):
            xt = (x + dx) % 4
            rows = pl.ds(pl.multiple_of(first_row(xt) + c * PIECE, PIECE), PIECE)
            for w, ref in enumerate((gate, up)):
                remote(ref.at[rows], wgu.at[c, x, w], gu_s.at[c], gu_r.at[c], z, xt)
        rows = pl.ds(pl.multiple_of(first_row(x) + c * PIECE, PIECE), PIECE)
        for w, ref in enumerate((gate, up)):
            pltpu.make_async_copy(ref.at[rows], wgu.at[c, x, w], gu_r.at[c]).start()

    def send_down(c):
        for dx in (2, 1, 3):
            xt = (x + dx) % 4
            rows = pl.ds(pl.multiple_of(first_row(xt) + c * PIECE, PIECE), PIECE)
            remote(down.at[rows], wd.at[c, x], d_s.at[c], d_r.at[c], z, xt)
        rows = pl.ds(pl.multiple_of(first_row(x) + c * PIECE, PIECE), PIECE)
        pltpu.make_async_copy(down.at[rows], wd.at[c, x], d_r.at[c]).start()

    load = pltpu.make_async_copy(tokens, tokv, t_c)
    load.start()
    send_gate_up(0)

    lanes = lax.broadcasted_iota(jnp.int32, (count, 128), 1)
    earlier = lax.broadcasted_iota(jnp.int32, (count, count), 0) >= (
        lax.broadcasted_iota(jnp.int32, (count, count), 1)
    )
    named = jnp.logical_or(routes[:, 0:1] == lanes, routes[:, 1:2] == lanes)
    order = contract(
        earlier.astype(jnp.bfloat16), named.astype(jnp.bfloat16), ((1,), (0,))
    ).astype(jnp.int32)
    mine = jnp.sum(jnp.where(jnp.logical_and(named, lanes == me), order, 0), axis=1, keepdims=True)
    placed = jnp.where(mine - 1 == lanes, 1.0, 0.0).T[0:slots].astype(jnp.bfloat16)
    load.wait()
    for q in range(4):
        cols = slice(q * wide, (q + 1) * wide)
        packed[:, cols] = contract(placed, tokv[:, cols], ((1,), (0,))).astype(packed.dtype)

    for hop in range(1, 16):
        other = (shard + hop) % 16
        remote(
            columns(other // 4), tokbuf.at[shard], tok_s.at[hop], tok_r.at[shard],
            other // 4, other % 4,
        )
    pltpu.make_async_copy(columns(z), tokbuf.at[shard], tok_r.at[shard]).start()
    for c in range(1, AHEAD):
        send_gate_up(c)

    for f in range(16):
        wait(tokbuf.at[f], tok_r.at[f])
        acc[pl.ds(f * slots, slots), :] = tokbuf[f].astype(jnp.float32)
    for g in range(4):
        rows = pl.ds(g * group, group)
        tok[rows, :] = acc[rows, :].astype(tok.dtype)
    acc[...] = jnp.zeros_like(acc)

    def partial_sums(i):
        slot = i % 4
        wait(wgu.at[i], gu_r.at[i])

        @pl.when(i >= 4)
        def _():
            wait(ps.at[slot], p_s.at[i - 4])

        def share(dz, w):
            rows = pl.ds(pl.multiple_of(((z + dz) % 4) * group, 16), group)
            total = contract(tok[rows, 0:PIECE], wgu[i, 0, w], ((1,), (1,)))
            for k in range(1, 4):
                total += contract(
                    tok[rows, k * PIECE : (k + 1) * PIECE], wgu[i, k, w], ((1,), (1,))
                )
            return total

        def emit(n, dz, w, dst, sem, to):
            ps[slot, n] = share(dz, w).astype(ps.dtype)
            remote(ps.at[slot, n], dst, p_s.at[i], sem, (z + to) % 4, x)

        emit(0, 2, 0, rl.at[i, 0], l_r.at[i], 1)
        emit(1, 2, 1, rl.at[i, 1], l_r.at[i], 3)
        emit(2, 1, 1, pr.at[i, 0], p_r.at[i], 1)
        emit(3, 3, 0, pr.at[i, 1], p_r.at[i], 3)
        keep[i % 2, 0] = share(1, 0)
        keep[i % 2, 1] = share(3, 1)
        own[i % 4, 0] = share(0, 0)
        own[i % 4, 1] = share(0, 1)

    def merge(j):
        wait(rl.at[j], l_r.at[j])
        for w, to in ((0, 1), (1, 3)):
            total = keep[j % 2, w] + rl[j, w].astype(jnp.float32)
            ps[j % 4, 4 + w] = total.astype(ps.dtype)
            remote(ps.at[j % 4, 4 + w], pr.at[j, 2 + w], p_s.at[j], p_r.at[j], (z + to) % 4, x)

    def activate(j):
        wait(pr.at[j], p_r.at[j])
        sums = [
            own[j % 4, w] + pr[j, 1 - w].astype(jnp.float32) + pr[j, 2 + w].astype(jnp.float32)
            for w in range(2)
        ]
        hidden = sums[0] / (1.0 + jnp.exp(-sums[0])) * sums[1]
        twice = jnp.logical_and(x == 3, j * PIECE < 4 * steps * PIECE - gate.shape[0])
        hidden = jnp.where(twice, jnp.zeros_like(hidden), hidden)
        hb[j, z] = hidden.astype(hb.dtype)
        for dz in (2, 1, 3):
            remote(hb.at[j, z], hb.at[j, z], h_s.at[j], h_r.at[j], (z + dz) % 4, x)

    def project(k):
        wait(hb.at[k, 0:3], h_r.at[k])
        wait(wd.at[k], d_r.at[k])
        for g in range(4):
            rows = pl.ds(g * group, group)
            for b in range(4):
                cols = slice(b * PIECE, (b + 1) * PIECE)
                acc[rows, cols] += contract(hb[k, g], wd[k, b], ((1,), (0,)))

    def step(i, carry):
        @pl.when(i + AHEAD < steps)
        def _():
            send_gate_up(i + AHEAD)

        @pl.when(i < steps)
        def _():
            send_down(i)
            partial_sums(i)

        @pl.when(jnp.logical_and(i >= 1, i < steps + 1))
        def _():
            merge(i - 1)

        @pl.when(jnp.logical_and(i >= 2, i < steps + 2))
        def _():
            activate(i - 2)

        @pl.when(i >= 3)
        def _():
            project(i - 3)

        return carry

    lax.fori_loop(0, steps + 3, step, 0)

    for dzb in (2, 1, 3, 0):
        zb = (z + dzb) % 4
        for dx in (2, 1, 3):
            xt = (x + dx) % 4
            rows = pl.ds(pl.multiple_of((zb * 4 + xt) * slots, 8), slots)
            osb[dzb, dx - 1] = acc[rows, :].astype(osb.dtype)
            remote(
                osb.at[dzb, dx - 1], orv.at[dzb, dx - 1],
                o_s.at[dzb * 3 + dx - 1], o_r.at[dzb * 3 + dx - 1], z, xt,
            )
    for dzb in (2, 1, 3, 0):
        zb = (z + dzb) % 4
        rows = pl.ds(pl.multiple_of((zb * 4 + x) * slots, 8), slots)
        total = acc[rows, :]
        for s in range(3):
            wait(orv.at[dzb, s], o_r.at[dzb * 3 + s])
            total += orv[dzb, s].astype(jnp.float32)
        for h in range(2):
            n = dzb * 2 + h
            fin[dzb, h] = total[:, h * half : (h + 1) * half].astype(fin.dtype)

            def leave(n=n, h=h, dzb=dzb, zb=zb):
                pltpu.make_async_remote_copy(
                    fin.at[dzb, h], frv.at[me], f_s.at[n], f_r.at[me],
                    device_id={"member": 2 * z + h, "fsdp": zb * 4 + x}, device_id_type=MESH,
                ).start()

            if dzb:
                leave()
            else:
                pl.when(me != 2 * z + h)(leave)

                @pl.when(me == 2 * z + h)
                def _():
                    pltpu.make_async_copy(fin.at[dzb, h], frv.at[me], f_r.at[me]).start()

    mixed = jnp.zeros((count, half), jnp.float32)
    for m in range(8):
        pick = jnp.where(
            jnp.logical_and(order[:, m : m + 1] - 1 == lanes, named[:, m : m + 1]), 1.0, 0.0
        )[:, 0:slots].astype(jnp.bfloat16)
        scale = jnp.sum(jnp.where(routes[...] == m, combine[...], 0.0), axis=1, keepdims=True)
        wait(frv.at[m], f_r.at[m])
        mixed += scale * contract(pick, frv[m], ((1,), (0,)))
    out[...] = mixed.astype(out.dtype)

    for dzb in range(4):
        for h in range(2):
            if dzb:
                wait(fin.at[dzb, h], f_s.at[dzb * 2 + h])
            else:
                @pl.when(me != 2 * z + h)
                def _():
                    wait(fin.at[dzb, h], f_s.at[dzb * 2 + h])
        for s in range(3):
            wait(osb.at[dzb, s], o_s.at[dzb * 3 + s])
    for hop in range(1, 16):
        wait(tokbuf.at[0], tok_s.at[hop])

    def finish(c, carry):
        wait(wgu.at[c, 0:3], gu_s.at[c])
        wait(wd.at[c, 0:3], d_s.at[c])
        wait(hb.at[c, 0:3], h_s.at[c])

        @pl.when(c >= steps - 4)
        def _():
            wait(ps.at[c % 4], p_s.at[c])

        return carry

    lax.fori_loop(0, steps, finish, 0)


def body(tokens, routes, combine, gate_weight, up_weight, down_weight):
    count, features = tokens.shape
    experts = lax.axis_size("member")
    gate, up, down = gate_weight[0], up_weight[0], down_weight[0]
    slots, wide, half = 3 * count // experts, features // 4, features // 8
    rows = 16 * slots
    steps = -(-gate.shape[0] // (4 * PIECE))
    bf16, f32 = jnp.bfloat16, jnp.float32
    dma = pltpu.SemaphoreType.DMA
    whole = pl.BlockSpec(memory_space=pltpu.VMEM)
    away = pl.BlockSpec(memory_space=pl.ANY)
    part = (rows // 4, PIECE)
    return pl.pallas_call(
        kernel,
        out_shape=jax.ShapeDtypeStruct((count, half), bf16),
        in_specs=[away, whole, whole, away, away, away],
        out_specs=whole,
        scratch_shapes=[
            pltpu.VMEM((count, features), bf16),
            pltpu.VMEM((slots, features), bf16),
            pltpu.VMEM((16, slots, wide), bf16),
            pltpu.VMEM((rows, wide), bf16),
            pltpu.VMEM((rows, wide), f32),
            pltpu.VMEM((steps, 4, 2, PIECE, PIECE), bf16),
            pltpu.VMEM((steps, 4, PIECE, PIECE), bf16),
            pltpu.VMEM((4, 6) + part, bf16),
            pltpu.VMEM((steps, 2) + part, bf16),
            pltpu.VMEM((steps, 4) + part, bf16),
            pltpu.VMEM((4, 2) + part, f32),
            pltpu.VMEM((2, 2) + part, f32),
            pltpu.VMEM((steps, 4) + part, bf16),
            pltpu.VMEM((4, 3, slots, wide), bf16),
            pltpu.VMEM((4, 3, slots, wide), bf16),
            pltpu.VMEM((4, 2, slots, half), bf16),
            pltpu.VMEM((8, slots, half), bf16),
            dma(()), dma((16,)), dma((16,)),
            dma((steps,)), dma((steps,)), dma((steps,)), dma((steps,)),
            dma((steps,)), dma((steps,)), dma((steps,)), dma((steps,)), dma((steps,)),
            dma((12,)), dma((12,)), dma((8,)), dma((8,)),
        ],
        compiler_params=pltpu.CompilerParams(
            has_side_effects=True, vmem_limit_bytes=67043328
        ),
    )(tokens, routes, combine, gate, up, down)


def solution(mesh):
    placed = (
        P("fsdp", None),
        P("fsdp", None),
        P("fsdp", None),
        P("member", None, "fsdp"),
        P("member", None, "fsdp"),
        P("member", None, "fsdp"),
    )
    return jax.shard_map(
        body, mesh=mesh, in_specs=placed, out_specs=P("fsdp", "member"), check_vma=False
    )
```

time: 338 us -> 292 us (0.86)
  Pallas kernels: 323 us -> 285 us
  matrix products: 6.29 us -> 0 us
    pallas_call x1, Pallas kernels: 323 us -> 285 us  [body(): pl.pallas_call(kernel, out_shape=jax.ShapeDtypeStruct((count, half), bf16...]
    dot_general x3 -> x0, matrix products: 6.29 us -> none  [the longest x2 3.55 us: body(): jnp.dot(pick, rows, preferred_element_type=jnp.float32)]
    unnamed x0 -> x3, local copies, waits for them, and re-layouts: none -> 4.5 us
where the time goes in v2:
time: 292 us; the launch traced here: 290 us
  Pallas kernels  285 us (98%)
  local copies, waits for them, and re-layouts  4.5 us (2%)
    pallas_call x1, Pallas kernels, body(): pl.pallas_call(kernel, out_shape=jax.ShapeDtypeStruct((count, half), bf16...  285 us

profile of v2, /device:TPU:0, one launch (start us, length us, event | category | flops | bytes accessed | tf_op | source)
XLA Modules:
  0.0 290.0 jit_solution(5761802418965833317)
XLA Ops:
  0.0 1.4 copy.7.routes
  1.4 1.4 copy.8.combine
  2.9 285.5 %shard_map.64 = bf16[192,512]{1,0:T(8,128)(2,1)} custom-call(bf16[192,4096]{1,0:T(8,128)(2,1)} %tokens.1, s32[192,2]{1,0:T(8,128)} %copy.7.routes, f32[192,2]{1,0:T(8,128)} %copy.8.combine, bf16[11008,256]{1,0:T(8,128)(2,1)} %bitcast.3, bf16[11008,256]{1,0:T(8,128)(2,1)} %bitcast.4, bf16[11008,256]{1,0:T(8,128)(2,1)} %bitcast.5), custom_call_target="tpu_custom_call" | custom-call | tf_op jit(solution)/shard_map/pallas_call | solution.py:271
  288.4 1.6 copy.10

commit v3 on v2

--- a/solution.py
+++ b/solution.py
@@ -17,7 +17,7 @@
 def kernel(
     tokens, routes, combine, gate, up, down, out,
     tokv, packed, tokbuf, tok, acc, wgu, wd, ps, rl, pr, own, keep, hb, osb, orv, fin, frv,
-    t_c, tok_s, tok_r, gu_s, gu_r, d_s, d_r, p_s, l_r, p_r, h_s, h_r, o_s, o_r, f_s, f_r,
+    t_c, tok_s, tok_r, gu_s, gu_r, d_s, d_r, p_s, l_r, p_r, h_s, h_r, q_s, q_r, o_s, o_r, f_s, f_r,
 ):
     steps = wgu.shape[0]
     slots = packed.shape[0]
@@ -29,8 +29,16 @@
     shard = lax.axis_index("fsdp")
     z, x = shard // 4, shard % 4
 
-    def first_row(xt):
-        return xt * (steps * PIECE) - (xt // 3) * (4 * steps * PIECE - gate.shape[0])
+    share_rows = gate.shape[0] // 4
+    short = share_rows - (steps - 1) * PIECE
+
+    def span(xt, c):
+        if isinstance(c, int) and c == 0:
+            return pl.ds(pl.multiple_of(xt * share_rows, 64), short)
+        return pl.ds(pl.multiple_of(xt * share_rows + short + (c - 1) * PIECE, 64), PIECE)
+
+    def filled(ref, c):
+        return ref.at[0:short] if isinstance(c, int) and c == 0 else ref
 
     def wait(ref, sem):
         pltpu.make_async_copy(ref, ref, sem).wait()
@@ -46,24 +54,40 @@
     def send_gate_up(c):
         for dx in (2, 1, 3):
             xt = (x + dx) % 4
-            rows = pl.ds(pl.multiple_of(first_row(xt) + c * PIECE, PIECE), PIECE)
             for w, ref in enumerate((gate, up)):
-                remote(ref.at[rows], wgu.at[c, x, w], gu_s.at[c], gu_r.at[c], z, xt)
-        rows = pl.ds(pl.multiple_of(first_row(x) + c * PIECE, PIECE), PIECE)
+                remote(
+                    ref.at[span(xt, c)], filled(wgu.at[c, x, w], c),
+                    gu_s.at[c], gu_r.at[c], z, xt,
+                )
         for w, ref in enumerate((gate, up)):
-            pltpu.make_async_copy(ref.at[rows], wgu.at[c, x, w], gu_r.at[c]).start()
+            pltpu.make_async_copy(
+                ref.at[span(x, c)], filled(wgu.at[c, x, w], c), gu_r.at[c]
+            ).start()
 
     def send_down(c):
         for dx in (2, 1, 3):
             xt = (x + dx) % 4
-            rows = pl.ds(pl.multiple_of(first_row(xt) + c * PIECE, PIECE), PIECE)
-            remote(down.at[rows], wd.at[c, x], d_s.at[c], d_r.at[c], z, xt)
-        rows = pl.ds(pl.multiple_of(first_row(x) + c * PIECE, PIECE), PIECE)
-        pltpu.make_async_copy(down.at[rows], wd.at[c, x], d_r.at[c]).start()
+            remote(down.at[span(xt, c)], filled(wd.at[c, x], c), d_s.at[c], d_r.at[c], z, xt)
+        pltpu.make_async_copy(down.at[span(x, c)], filled(wd.at[c, x], c), d_r.at[c]).start()
+
+    barrier = pltpu.get_barrier_semaphore()
+    for hop in range(1, 16):
+        pl.semaphore_signal(
+            barrier, inc=1, device_id={"fsdp": (shard + hop) % 16}, device_id_type=MESH
+        )
+    inside = me // 2 == z
+    for m in range(8):
+        @pl.when(jnp.logical_not(jnp.logical_and(inside, me == m)))
+        def _():
+            pl.semaphore_signal(
+                barrier, inc=1, device_id={"member": m, "fsdp": (me // 2) * 4 + x},
+                device_id_type=MESH,
+            )
 
     load = pltpu.make_async_copy(tokens, tokv, t_c)
     load.start()
-    send_gate_up(0)
+    wgu[0, :, :, short:, :] = jnp.zeros((4, 2, PIECE - short, PIECE), wgu.dtype)
+    wd[0, :, short:, :] = jnp.zeros((4, PIECE - short, PIECE), wd.dtype)
 
     lanes = lax.broadcasted_iota(jnp.int32, (count, 128), 1)
     earlier = lax.broadcasted_iota(jnp.int32, (count, count), 0) >= (
@@ -80,31 +104,55 @@
         cols = slice(q * wide, (q + 1) * wide)
         packed[:, cols] = contract(placed, tokv[:, cols], ((1,), (0,))).astype(packed.dtype)
 
-    for hop in range(1, 16):
-        other = (shard + hop) % 16
-        remote(
-            columns(other // 4), tokbuf.at[shard], tok_s.at[hop], tok_r.at[shard],
-            other // 4, other % 4,
-        )
-    pltpu.make_async_copy(columns(z), tokbuf.at[shard], tok_r.at[shard]).start()
-    for c in range(1, AHEAD):
+    @pl.when(inside)
+    def _():
+        pl.semaphore_wait(barrier, 22)
+
+    @pl.when(jnp.logical_not(inside))
+    def _():
+        pl.semaphore_wait(barrier, 23)
+
+    def spread(dz):
+        zt = (z + dz) % 4
+        for dx in (2, 1, 3, 0):
+            xt = (x + dx) % 4
+            if dz or dx:
+                remote(
+                    columns(zt), tokbuf.at[shard], tok_s.at[dz * 4 + dx], tok_r.at[shard], zt, xt
+                )
+            else:
+                pltpu.make_async_copy(columns(z), tokbuf.at[shard], tok_r.at[shard]).start()
+
+    spread(2)
+    send_gate_up(0)
+    for dz in (1, 3, 0):
+        spread(dz)
+    for c in range(1, AHEAD + 1):
         send_gate_up(c)
-
-    for f in range(16):
-        wait(tokbuf.at[f], tok_r.at[f])
-        acc[pl.ds(f * slots, slots), :] = tokbuf[f].astype(jnp.float32)
-    for g in range(4):
-        rows = pl.ds(g * group, group)
+    send_down(0)
+
+    def unpack(dz):
+        zt = (z + dz) % 4
+        for k in range(4):
+            f = zt * 4 + k
+            wait(tokbuf.at[f], tok_r.at[f])
+            acc[pl.ds(pl.multiple_of(f * slots, 8), slots), :] = tokbuf[f].astype(jnp.float32)
+        rows = pl.ds(pl.multiple_of(zt * group, 16), group)
         tok[rows, :] = acc[rows, :].astype(tok.dtype)
-    acc[...] = jnp.zeros_like(acc)
 
     def partial_sums(i):
         slot = i % 4
-        wait(wgu.at[i], gu_r.at[i])
-
-        @pl.when(i >= 4)
-        def _():
-            wait(ps.at[slot], p_s.at[i - 4])
+        first = isinstance(i, int)
+        ready = (lambda dz: unpack(dz)) if first else (lambda dz: None)
+        if first:
+            ready(2)
+            wait(wgu.at[0, :, :, 0:short], gu_r.at[0])
+        else:
+            wait(wgu.at[i], gu_r.at[i])
+
+            @pl.when(i >= 4)
+            def _():
+                wait(ps.at[slot], p_s.at[i - 4])
 
         def share(dz, w):
             rows = pl.ds(pl.multiple_of(((z + dz) % 4) * group, 16), group)
@@ -121,8 +169,11 @@
 
         emit(0, 2, 0, rl.at[i, 0], l_r.at[i], 1)
         emit(1, 2, 1, rl.at[i, 1], l_r.at[i], 3)
+        ready(1)
         emit(2, 1, 1, pr.at[i, 0], p_r.at[i], 1)
+        ready(3)
         emit(3, 3, 0, pr.at[i, 1], p_r.at[i], 3)
+        ready(0)
         keep[i % 2, 0] = share(1, 0)
         keep[i % 2, 1] = share(3, 1)
         own[i % 4, 0] = share(0, 0)
@@ -142,15 +193,27 @@
             for w in range(2)
         ]
         hidden = sums[0] / (1.0 + jnp.exp(-sums[0])) * sums[1]
-        twice = jnp.logical_and(x == 3, j * PIECE < 4 * steps * PIECE - gate.shape[0])
-        hidden = jnp.where(twice, jnp.zeros_like(hidden), hidden)
         hb[j, z] = hidden.astype(hb.dtype)
-        for dz in (2, 1, 3):
+        for dz in (1, 3):
             remote(hb.at[j, z], hb.at[j, z], h_s.at[j], h_r.at[j], (z + dz) % 4, x)
 
+    def forward(j):
+        wait(hb.at[j, 0:2], h_r.at[j])
+        for dz, lo in ((1, 0), (3, group // 2)):
+            piece = hb.at[j, (z - dz + 4) % 4, pl.ds(lo, group // 2)]
+            remote(piece, piece, q_s.at[j], q_r.at[j], (z + dz) % 4, x)
+
     def project(k):
-        wait(hb.at[k, 0:3], h_r.at[k])
-        wait(wd.at[k], d_r.at[k])
+        wait(hb.at[k, 0], q_r.at[k])
+
+        @pl.when(k == 0)
+        def _():
+            wait(wd.at[0, :, 0:short], d_r.at[0])
+
+        @pl.when(k > 0)
+        def _():
+            wait(wd.at[k], d_r.at[k])
+
         for g in range(4):
             rows = pl.ds(g * group, group)
             for b in range(4):
@@ -167,7 +230,7 @@
             send_down(i)
             partial_sums(i)
 
-        @pl.when(jnp.logical_and(i >= 1, i < steps + 1))
+        @pl.when(i < steps + 1)
         def _():
             merge(i - 1)
 
@@ -175,13 +238,19 @@
         def _():
             activate(i - 2)
 
-        @pl.when(i >= 3)
-        def _():
-            project(i - 3)
+        @pl.when(jnp.logical_and(i >= 3, i < steps + 3))
+        def _():
+            forward(i - 3)
+
+        @pl.when(i >= 4)
+        def _():
+            project(i - 4)
 
         return carry
 
-    lax.fori_loop(0, steps + 3, step, 0)
+    partial_sums(0)
+    acc[...] = jnp.zeros_like(acc)
+    lax.fori_loop(1, steps + 4, step, 0)
 
     for dzb in (2, 1, 3, 0):
         zb = (z + dzb) % 4
@@ -241,11 +310,17 @@
             wait(osb.at[dzb, s], o_s.at[dzb * 3 + s])
     for hop in range(1, 16):
         wait(tokbuf.at[0], tok_s.at[hop])
+    wait(wgu.at[0, 0:3, :, 0:short], gu_s.at[0])
+    wait(wd.at[0, 0:3, 0:short], d_s.at[0])
 
     def finish(c, carry):
-        wait(wgu.at[c, 0:3], gu_s.at[c])
-        wait(wd.at[c, 0:3], d_s.at[c])
-        wait(hb.at[c, 0:3], h_s.at[c])
+        @pl.when(c >= 1)
+        def _():
+            wait(wgu.at[c, 0:3], gu_s.at[c])
+            wait(wd.at[c, 0:3], d_s.at[c])
+
+        wait(hb.at[c, 0:2], h_s.at[c])
+        wait(hb.at[c, 0], q_s.at[c])
 
         @pl.when(c >= steps - 4)
         def _():
@@ -294,10 +369,11 @@
             dma(()), dma((16,)), dma((16,)),
             dma((steps,)), dma((steps,)), dma((steps,)), dma((steps,)),
             dma((steps,)), dma((steps,)), dma((steps,)), dma((steps,)), dma((steps,)),
+            dma((steps,)), dma((steps,)),
             dma((12,)), dma((12,)), dma((8,)), dma((8,)),
         ],
         compiler_params=pltpu.CompilerParams(
-            has_side_effects=True, vmem_limit_bytes=67043328
+            has_side_effects=True, collective_id=0, vmem_limit_bytes=67043328
         ),
     )(tokens, routes, combine, gate, up, down)
 

time: 292 us -> 276 us (0.945)
  Pallas kernels: 285 us -> 270 us
    pallas_call x1, Pallas kernels: 285 us -> 270 us  [body(): pl.pallas_call(kernel, out_shape=jax.ShapeDtypeStruct((count, half), bf16...]
where the time goes in v3:
time: 276 us; the launch traced here: 275 us
  Pallas kernels  270 us (98%)
  local copies, waits for them, and re-layouts  4.5 us (2%)
    pallas_call x1, Pallas kernels, body(): pl.pallas_call(kernel, out_shape=jax.ShapeDtypeStruct((count, half), bf16...  270 us

profile of v3, /device:TPU:0, one launch (start us, length us, event | category | flops | bytes accessed | tf_op | source)
XLA Modules:
  0.0 274.6 jit_solution(9061828579667707015)
XLA Ops:
  0.0 1.4 copy.7.routes
  1.4 1.4 copy.8.combine
  2.9 270.1 %shard_map.64 = bf16[192,512]{1,0:T(8,128)(2,1)} custom-call(bf16[192,4096]{1,0:T(8,128)(2,1)} %tokens.1, s32[192,2]{1,0:T(8,128)} %copy.7.routes, f32[192,2]{1,0:T(8,128)} %copy.8.combine, bf16[11008,256]{1,0:T(8,128)(2,1)} %bitcast.3, bf16[11008,256]{1,0:T(8,128)(2,1)} %bitcast.4, bf16[11008,256]{1,0:T(8,128)(2,1)} %bitcast.5), custom_call_target="tpu_custom_call" | custom-call | tf_op jit(solution)/shard_map/pallas_call | solution.py:346
  273.0 1.6 copy.10

commit v4 on v3

--- a/solution.py
+++ b/solution.py
@@ -6,7 +6,8 @@
 from jax.sharding import PartitionSpec as P
 
 PIECE = 256
-AHEAD = 3
+AHEAD = 6
+LAG = 7
 MESH = pl.DeviceIdType.MESH
 
 
@@ -93,7 +94,13 @@
     earlier = lax.broadcasted_iota(jnp.int32, (count, count), 0) >= (
         lax.broadcasted_iota(jnp.int32, (count, count), 1)
     )
-    named = jnp.logical_or(routes[:, 0:1] == lanes, routes[:, 1:2] == lanes)
+    line = lax.broadcasted_iota(jnp.int32, (128, count), 0)
+    table = jnp.where(line == 0, routes[0:1, :], routes[1:2, :]).astype(jnp.float32)
+    table = jnp.where(line == 2, combine[0:1, :], table)
+    table = jnp.where(line == 3, combine[1:2, :], table).T
+    pair = [table[:, k : k + 1].astype(jnp.int32) for k in range(2)]
+    share_of = [table[:, k : k + 1] for k in (2, 3)]
+    named = jnp.logical_or(pair[0] == lanes, pair[1] == lanes)
     order = contract(
         earlier.astype(jnp.bfloat16), named.astype(jnp.bfloat16), ((1,), (0,))
     ).astype(jnp.int32)
@@ -112,30 +119,29 @@
     def _():
         pl.semaphore_wait(barrier, 23)
 
-    def spread(dz):
+    for dz in (2, 1, 3):
         zt = (z + dz) % 4
-        for dx in (2, 1, 3, 0):
-            xt = (x + dx) % 4
-            if dz or dx:
-                remote(
-                    columns(zt), tokbuf.at[shard], tok_s.at[dz * 4 + dx], tok_r.at[shard], zt, xt
-                )
-            else:
-                pltpu.make_async_copy(columns(z), tokbuf.at[shard], tok_r.at[shard]).start()
-
-    spread(2)
+        remote(columns(zt), tokbuf.at[shard], tok_s.at[dz], tok_r.at[shard], zt, x)
+    pltpu.make_async_copy(columns(z), tokbuf.at[shard], tok_r.at[shard]).start()
     send_gate_up(0)
-    for dz in (1, 3, 0):
-        spread(dz)
+    for dz in (2, 1, 3, 0):
+        f = ((z + dz) % 4) * 4 + x
+        wait(tokbuf.at[f], tok_r.at[f])
+        for dx in (2, 1, 3):
+            remote(
+                tokbuf.at[f], tokbuf.at[f], tok_s.at[3 + dz * 3 + dx], tok_r.at[f],
+                z, (x + dx) % 4,
+            )
     for c in range(1, AHEAD + 1):
         send_gate_up(c)
     send_down(0)
 
     def unpack(dz):
         zt = (z + dz) % 4
-        for k in range(4):
-            f = zt * 4 + k
-            wait(tokbuf.at[f], tok_r.at[f])
+        for dx in (0, 1, 3, 2):
+            f = zt * 4 + (x + dx) % 4
+            if dx:
+                wait(tokbuf.at[f], tok_r.at[f])
             acc[pl.ds(pl.multiple_of(f * slots, 8), slots), :] = tokbuf[f].astype(jnp.float32)
         rows = pl.ds(pl.multiple_of(zt * group, 16), group)
         tok[rows, :] = acc[rows, :].astype(tok.dtype)
@@ -242,15 +248,15 @@
         def _():
             forward(i - 3)
 
-        @pl.when(i >= 4)
-        def _():
-            project(i - 4)
+        @pl.when(i >= LAG)
+        def _():
+            project(i - LAG)
 
         return carry
 
     partial_sums(0)
     acc[...] = jnp.zeros_like(acc)
-    lax.fori_loop(1, steps + 4, step, 0)
+    lax.fori_loop(1, steps + LAG, step, 0)
 
     for dzb in (2, 1, 3, 0):
         zb = (z + dzb) % 4
@@ -293,7 +299,9 @@
         pick = jnp.where(
             jnp.logical_and(order[:, m : m + 1] - 1 == lanes, named[:, m : m + 1]), 1.0, 0.0
         )[:, 0:slots].astype(jnp.bfloat16)
-        scale = jnp.sum(jnp.where(routes[...] == m, combine[...], 0.0), axis=1, keepdims=True)
+        scale = jnp.where(pair[0] == m, share_of[0], 0.0) + jnp.where(
+            pair[1] == m, share_of[1], 0.0
+        )
         wait(frv.at[m], f_r.at[m])
         mixed += scale * contract(pick, frv[m], ((1,), (0,)))
     out[...] = mixed.astype(out.dtype)
@@ -375,7 +383,7 @@
         compiler_params=pltpu.CompilerParams(
             has_side_effects=True, collective_id=0, vmem_limit_bytes=67043328
         ),
-    )(tokens, routes, combine, gate, up, down)
+    )(tokens, routes.T, combine.T, gate, up, down)
 
 
 def solution(mesh):

time: 276 us -> 265 us (0.960)
  Pallas kernels: 270 us -> 261 us
  local copies, waits for them, and re-layouts: 4.5 us -> 1.62 us
    pallas_call x1, Pallas kernels: 270 us -> 261 us  [body(): pl.pallas_call(kernel, out_shape=jax.ShapeDtypeStruct((count, half), bf16...]
    unnamed x3 -> x1, local copies, waits for them, and re-layouts: 4.5 us -> 1.62 us
where the time goes in v4:
time: 265 us; the launch traced here: 263 us
  Pallas kernels  261 us (98%)
    pallas_call x1, Pallas kernels, body(): pl.pallas_call(kernel, out_shape=jax.ShapeDtypeStruct((count, half), bf16...  261 us

profile of v4, /device:TPU:0, one launch (start us, length us, event | category | flops | bytes accessed | tf_op | source)
XLA Modules:
  0.0 262.6 jit_solution(12408833586614549300)
XLA Ops:
  0.0 260.9 %shard_map.64 = bf16[192,512]{1,0:T(8,128)(2,1)} custom-call(bf16[192,4096]{1,0:T(8,128)(2,1)} %tokens.1, s32[2,192]{1,0:T(2,128)} %bitcast.8, f32[2,192]{1,0:T(2,128)} %bitcast.9, bf16[11008,256]{1,0:T(8,128)(2,1)} %bitcast.5, bf16[11008,256]{1,0:T(8,128)(2,1)} %bitcast.6, bf16[11008,256]{1,0:T(8,128)(2,1)} %bitcast.7), custom_call_target="tpu_custom_call" | custom-call | tf_op jit(solution)/shard_map/pallas_call | solution.py:354
  260.9 1.6 copy.8

commit v5 on v4

--- a/solution.py
+++ b/solution.py
@@ -18,7 +18,7 @@
 def kernel(
     tokens, routes, combine, gate, up, down, out,
     tokv, packed, tokbuf, tok, acc, wgu, wd, ps, rl, pr, own, keep, hb, osb, orv, fin, frv,
-    t_c, tok_s, tok_r, gu_s, gu_r, d_s, d_r, p_s, l_r, p_r, h_s, h_r, q_s, q_r, o_s, o_r, f_s, f_r,
+    t_c, tok_s, tok_r, fw_s, fw_r, gu_s, gu_r, d_s, d_r, p_s, l_r, p_r, h_s, h_r, q_s, q_r, o_s, o_r, f_s, f_r,
 ):
     steps = wgu.shape[0]
     slots = packed.shape[0]
@@ -127,20 +127,28 @@
     for dz in (2, 1, 3, 0):
         f = ((z + dz) % 4) * 4 + x
         wait(tokbuf.at[f], tok_r.at[f])
-        for dx in (2, 1, 3):
+        for dx in (2, 1, 3) if dz == 2 else (1, 3):
             remote(
                 tokbuf.at[f], tokbuf.at[f], tok_s.at[3 + dz * 3 + dx], tok_r.at[f],
                 z, (x + dx) % 4,
             )
-    for c in range(1, AHEAD + 1):
-        send_gate_up(c)
-    send_down(0)
+    send_gate_up(1)
+
+    def hand_on(dz):
+        for n, dx in enumerate((1, 3)):
+            f = ((z + dz) % 4) * 4 + (x - dx + 4) % 4
+            wait(tokbuf.at[f], tok_r.at[f])
+            piece = tokbuf.at[f, :, n * (wide // 2) : (n + 1) * (wide // 2)]
+            remote(piece, piece, fw_s.at[dz * 2 + n], fw_r.at[dz * 2 + n], z, (x + dx) % 4)
 
     def unpack(dz):
         zt = (z + dz) % 4
         for dx in (0, 1, 3, 2):
             f = zt * 4 + (x + dx) % 4
-            if dx:
+            if dz != 2 and dx == 2:
+                for n in range(2):
+                    wait(tokbuf.at[f, :, 0 : wide // 2], fw_r.at[dz * 2 + n])
+            elif dz == 2 and dx:
                 wait(tokbuf.at[f], tok_r.at[f])
             acc[pl.ds(pl.multiple_of(f * slots, 8), slots), :] = tokbuf[f].astype(jnp.float32)
         rows = pl.ds(pl.multiple_of(zt * group, 16), group)
@@ -175,6 +183,12 @@
 
         emit(0, 2, 0, rl.at[i, 0], l_r.at[i], 1)
         emit(1, 2, 1, rl.at[i, 1], l_r.at[i], 3)
+        if first:
+            for dz in (1, 3, 0):
+                hand_on(dz)
+            for c in range(2, AHEAD + 1):
+                send_gate_up(c)
+            send_down(0)
         ready(1)
         emit(2, 1, 1, pr.at[i, 0], p_r.at[i], 1)
         ready(3)
@@ -316,8 +330,11 @@
                     wait(fin.at[dzb, h], f_s.at[dzb * 2 + h])
         for s in range(3):
             wait(osb.at[dzb, s], o_s.at[dzb * 3 + s])
-    for hop in range(1, 16):
+    for hop in (1, 2, 3) + tuple(3 + dz * 3 + dx for dz in range(4) for dx in (1, 3)) + (11,):
         wait(tokbuf.at[0], tok_s.at[hop])
+    for dz in (1, 3, 0):
+        for n in range(2):
+            wait(tokbuf.at[0, :, 0 : wide // 2], fw_s.at[dz * 2 + n])
     wait(wgu.at[0, 0:3, :, 0:short], gu_s.at[0])
     wait(wd.at[0, 0:3, 0:short], d_s.at[0])
 
@@ -374,7 +391,7 @@
             pltpu.VMEM((4, 3, slots, wide), bf16),
             pltpu.VMEM((4, 2, slots, half), bf16),
             pltpu.VMEM((8, slots, half), bf16),
-            dma(()), dma((16,)), dma((16,)),
+            dma(()), dma((16,)), dma((16,)), dma((8,)), dma((8,)),
             dma((steps,)), dma((steps,)), dma((steps,)), dma((steps,)),
             dma((steps,)), dma((steps,)), dma((steps,)), dma((steps,)), dma((steps,)),
             dma((steps,)), dma((steps,)),

time: 265 us -> 260 us (0.981)
  Pallas kernels: 261 us -> 256 us
    pallas_call x1, Pallas kernels: 261 us -> 256 us  [body(): pl.pallas_call(kernel, out_shape=jax.ShapeDtypeStruct((count, half), bf16...]
where the time goes in v5:
time: 260 us; the launch traced here: 258 us
  Pallas kernels  256 us (98%)
    pallas_call x1, Pallas kernels, body(): pl.pallas_call(kernel, out_shape=jax.ShapeDtypeStruct((count, half), bf16...  256 us

profile of v5, /device:TPU:0, one launch (start us, length us, event | category | flops | bytes accessed | tf_op | source)
XLA Modules:
  0.0 257.7 jit_solution(17026954769571485534)
XLA Ops:
  0.0 256.1 %shard_map.64 = bf16[192,512]{1,0:T(8,128)(2,1)} custom-call(bf16[192,4096]{1,0:T(8,128)(2,1)} %tokens.1, s32[2,192]{1,0:T(2,128)} %bitcast.8, f32[2,192]{1,0:T(2,128)} %bitcast.9, bf16[11008,256]{1,0:T(8,128)(2,1)} %bitcast.5, bf16[11008,256]{1,0:T(8,128)(2,1)} %bitcast.6, bf16[11008,256]{1,0:T(8,128)(2,1)} %bitcast.7), custom_call_target="tpu_custom_call" | custom-call | tf_op jit(solution)/shard_map/pallas_call | solution.py:371
  256.1 1.6 copy.8

commit v6 on v5

--- a/solution.py
+++ b/solution.py
@@ -262,15 +262,22 @@
         def _():
             forward(i - 3)
 
+        late = i // steps
+        k = i - LAG + late * (i - steps)
+
         @pl.when(i >= LAG)
         def _():
-            project(i - LAG)
+            project(k)
+
+        @pl.when(jnp.logical_and(i >= steps, k + 1 < steps))
+        def _():
+            project(k + 1)
 
         return carry
 
     partial_sums(0)
     acc[...] = jnp.zeros_like(acc)
-    lax.fori_loop(1, steps + LAG, step, 0)
+    lax.fori_loop(1, steps + (LAG + 1) // 2, step, 0)
 
     for dzb in (2, 1, 3, 0):
         zb = (z + dzb) % 4

time: 260 us -> 260 us (level)
  no operation moved by 1% of the time
where the time goes in v6:
time: 260 us; the launch traced here: 258 us
  Pallas kernels  256 us (98%)
    pallas_call x1, Pallas kernels, body(): pl.pallas_call(kernel, out_shape=jax.ShapeDtypeStruct((count, half), bf16...  256 us

profile of v6, /device:TPU:0, one launch (start us, length us, event | category | flops | bytes accessed | tf_op | source)
XLA Modules:
  0.0 257.7 jit_solution(8942004361265179794)
XLA Ops:
  0.0 256.1 %shard_map.64 = bf16[192,512]{1,0:T(8,128)(2,1)} custom-call(bf16[192,4096]{1,0:T(8,128)(2,1)} %tokens.1, s32[2,192]{1,0:T(2,128)} %bitcast.8, f32[2,192]{1,0:T(2,128)} %bitcast.9, bf16[11008,256]{1,0:T(8,128)(2,1)} %bitcast.5, bf16[11008,256]{1,0:T(8,128)(2,1)} %bitcast.6, bf16[11008,256]{1,0:T(8,128)(2,1)} %bitcast.7), custom_call_target="tpu_custom_call" | custom-call | tf_op jit(solution)/shard_map/pallas_call | solution.py:378
  256.1 1.6 copy.8
